TPU v7x, 32 devices: a whole 2x2x4 slice. The times are simulated.
32 devices in a mesh: head: 4 (over z), span: 8 (over y, x, core).
Axes of the slice: x: 2, y: 2, z: 4, core: 2. Of those that a mesh axis runs over, the one named last changes fastest.
Arguments:
- queries: bfloat16 [4096, 2048], P(('span', 'head')), may hold values from -6 to 6
- keys: bfloat16 [4096, 2048], P(('span', 'head')), may hold values from -6 to 6
- values: bfloat16 [4096, 2048], P(('span', 'head')), may hold values from -6 to 6
- out_grad: bfloat16 [4096, 2048], P(('span', 'head')), may hold values from -6 to 6
Outputs:
- attn_out: bfloat16 [4096, 2048], P(('span', 'head'))
- query_gradient: bfloat16 [4096, 2048], P(('span', 'head'))
- grad_key: bfloat16 [4096, 2048], P(('span', 'head'))
- grad_value: bfloat16 [4096, 2048], P(('span', 'head'))
All inputs are finite; a program needn't handle non-finite values.
Results may differ from a plain program's by a relative error of at most 0.0058.
Values may be sent and summed in bfloat16 or wider, within the bound.
No kernel may reach another device: no remote copies, remote signals or barrier semaphores. Data moves between devices by JAX's collectives and lax.ppermute only.
A program may use at most 64 MiB of HBM per device.

v0:
```python
import jax
import jax.numpy as jnp
from jax import lax
from jax.sharding import PartitionSpec as P

HEADS = 16
DH = 128


def block_work(queries, keys, values, scaled, position_scale, forward_narrow, back_low):
    length = queries.shape[0]
    head_count = queries.shape[1]
    head_width = queries.shape[2]
    row_count = min(512, length)
    outputs = []
    query_grads = []
    key_acc = jnp.zeros((length, head_count, head_width), jnp.float32)
    value_acc = jnp.zeros((length, head_count, head_width), jnp.float32)
    for block_index in range(length // row_count):
        start_row = block_index * row_count
        end_row = start_row + row_count
        query_lines = queries[start_row:end_row]
        scaled_lines = scaled[start_row:end_row]
        key_cols = keys[:end_row]
        value_cols = values[:end_row]
        row_pos = start_row + lax.iota(jnp.int32, row_count)
        col_pos = lax.iota(jnp.int32, end_row)
        causal = col_pos[None, :] <= row_pos[:, None]
        raw_scores = jnp.einsum(
            "tnd,snd->nts", query_lines, key_cols, preferred_element_type=jnp.float32
        )
        scores = jnp.where(causal[None], raw_scores, 0.0).astype(jnp.bfloat16)
        raw_grads = jnp.einsum(
            "tnd,snd->nts", scaled_lines, value_cols, preferred_element_type=jnp.float32
        )
        score_gradient = jnp.where(causal[None], raw_grads, 0.0).astype(jnp.bfloat16)
        local_out = jnp.einsum(
            "epa,aev->pev", scores, value_cols, preferred_element_type=jnp.float32
        )
        carried_result = jnp.einsum(
            "rwb,wbo->rwo", query_lines, forward_narrow, preferred_element_type=jnp.float32
        )
        row_scale = position_scale[start_row:end_row]
        outputs.append(
            ((local_out + carried_result) * row_scale[:, None, None]).astype(jnp.bfloat16)
        )
        local_query = jnp.einsum(
            "epa,aev->pev", score_gradient, key_cols, preferred_element_type=jnp.float32
        )
        carried_query = jnp.einsum(
            "hsx,smx->hsm", scaled_lines, forward_narrow, preferred_element_type=jnp.float32
        )
        query_grads.append((local_query + carried_query).astype(jnp.bfloat16))
        key_acc = key_acc.at[:end_row].add(
            jnp.einsum(
                "nts,tnd->snd", score_gradient, query_lines, preferred_element_type=jnp.float32
            )
        )
        value_acc = value_acc.at[:end_row].add(
            jnp.einsum("nts,tnd->snd", scores, scaled_lines, preferred_element_type=jnp.float32)
        )
    grad_key = (
        key_acc + jnp.einsum("snv,nvk->snk", values, back_low, preferred_element_type=jnp.float32)
    ).astype(jnp.bfloat16)
    grad_value = (
        value_acc + jnp.einsum("snk,nvk->snv", keys, back_low, preferred_element_type=jnp.float32)
    ).astype(jnp.bfloat16)
    return (
        jnp.concatenate(outputs, axis=0),
        jnp.concatenate(query_grads, axis=0),
        grad_key,
        grad_value,
    )


def attend(pieces):
    queries = pieces[0][:, 0]
    keys = pieces[1][:, 0]
    values = pieces[2][:, 0]
    out_grad = pieces[3][:, 0]
    length = queries.shape[0]
    head_width = queries.shape[2]
    span_index = lax.axis_index("span")
    position = span_index * length + lax.iota(jnp.int32, length)
    position_scale = 1.0 / jnp.sqrt(jnp.float32(head_width) * (position + 1).astype(jnp.float32))
    scaled = (out_grad.astype(jnp.float32) * position_scale[:, None, None]).astype(jnp.bfloat16)
    forward_within = jnp.einsum("xgy,xgi->gyi", keys, values, preferred_element_type=jnp.float32)
    back_local = jnp.einsum("tnv,tnk->nvk", scaled, queries, preferred_element_type=jnp.float32)
    every_fwd, every_back = (
        lax.all_gather(forward_within[None], "span", axis=0, tiled=True),
        lax.all_gather(back_local[None], "span", axis=0, tiled=True),
    )
    block_order = lax.iota(jnp.int32, every_fwd.shape[0])
    lower_mask = (block_order < span_index).astype(jnp.float32)[:, None, None, None]
    upper_mask = (block_order > span_index).astype(jnp.float32)[:, None, None, None]
    fwd_state = jnp.sum(every_fwd * lower_mask, axis=0)
    back_state = jnp.sum(every_back * upper_mask, axis=0)
    forward_narrow = fwd_state.astype(jnp.bfloat16)
    back_low = back_state.astype(jnp.bfloat16)
    results = block_work(queries, keys, values, scaled, position_scale, forward_narrow, back_low)
    return (results[0][:, None], results[1][:, None], results[2][:, None], results[3][:, None])


def split_heads(matrix, group_count):
    return matrix.reshape(matrix.shape[0], group_count, HEADS // group_count, DH)


def merge_heads(grouped):
    return grouped.reshape(grouped.shape[0], HEADS * DH)


def shards(queries, keys, values, out_grad):
    group_count = lax.axis_size("head")
    results = attend(
        (
            lax.all_to_all(
                split_heads(queries, group_count), "head", split_axis=1, concat_axis=0, tiled=True
            ),
            lax.all_to_all(
                split_heads(keys, group_count), "head", split_axis=1, concat_axis=0, tiled=True
            ),
            lax.all_to_all(
                split_heads(values, group_count), "head", split_axis=1, concat_axis=0, tiled=True
            ),
            lax.all_to_all(
                split_heads(out_grad, group_count), "head", split_axis=1, concat_axis=0, tiled=True
            ),
        )
    )
    returned = (
        lax.all_to_all(results[0], "head", split_axis=0, concat_axis=1, tiled=True),
        lax.all_to_all(results[1], "head", split_axis=0, concat_axis=1, tiled=True),
        lax.all_to_all(results[2], "head", split_axis=0, concat_axis=1, tiled=True),
        lax.all_to_all(results[3], "head", split_axis=0, concat_axis=1, tiled=True),
    )
    return (
        merge_heads(returned[0]),
        merge_heads(returned[1]),
        merge_heads(returned[2]),
        merge_heads(returned[3]),
    )


def solution(mesh):
    return jax.shard_map(
        shards,
        mesh=mesh,
        in_specs=(
            P(("span", "head"), None),
            P(("span", "head"), None),
            P(("span", "head"), None),
            P(("span", "head"), None),
        ),
        out_specs=(
            P(("span", "head"), None),
            P(("span", "head"), None),
            P(("span", "head"), None),
            P(("span", "head"), None),
        ),
        check_vma=False,
    )
```

profile of v0, /device:TPU:0, one launch (start us, length us, event | category | flops | bytes accessed | tf_op | source)
XLA Modules:
  0.0 181.5 jit_solution(9970101980685170848)
XLA Ops:
  7.2 1.4 copy.49
  9.6 6.3 %all-to-all-start.1 = ((bf16[128,4,4,128]{3,0,2,1:T(8,128)(2,1)}), bf16[128,4,4,128]{3,0,2,1:T(8,128)(2,1)S(1)}, u32[]{:S(2)}, u32[]{:S(2)}) async-start(bf16[128,4,4,128]{3,0,2,1:T(8,128)(2,1)} %copy.50), calls=%async_computation.1 | async-start | bytes 1048576 | tf_op jit(solution)/shard_map/all_to_all | solution.py:119
  17.2 13.2 %all-to-all-done.1 = bf16[128,4,4,128]{3,0,2,1:T(8,128)(2,1)S(1)} async-done(((bf16[128,4,4,128]{3,0,2,1:T(8,128)(2,1)}), bf16[128,4,4,128]{3,0,2,1:T(8,128)(2,1)S(1)}, u32[]{:S(2)}, u32[]{:S(2)}) %all-to-all-start.1) | async-done | bytes 524320 | tf_op jit(solution)/shard_map/all_to_all | solution.py:119
  30.4 3.5 %all-to-all-start.2 = ((bf16[128,4,4,128]{3,0,2,1:T(8,128)(2,1)}), bf16[128,4,4,128]{3,0,2,1:T(8,128)(2,1)S(1)}, u32[]{:S(2)}, u32[]{:S(2)}) async-start(bf16[128,4,4,128]{3,0,2,1:T(8,128)(2,1)} %copy.53), calls=%async_computation.2 | async-start | bytes 1048576 | tf_op jit(solution)/shard_map/all_to_all | solution.py:122
  34.0 13.9 %all-to-all-done.2 = bf16[128,4,4,128]{3,0,2,1:T(8,128)(2,1)S(1)} async-done(((bf16[128,4,4,128]{3,0,2,1:T(8,128)(2,1)}), bf16[128,4,4,128]{3,0,2,1:T(8,128)(2,1)S(1)}, u32[]{:S(2)}, u32[]{:S(2)}) %all-to-all-start.2) | async-done | bytes 524320 | tf_op jit(solution)/shard_map/all_to_all | solution.py:122
  50.3 3.5 %all-to-all-start = ((bf16[128,4,4,128]{3,0,2,1:T(8,128)(2,1)}), bf16[128,4,4,128]{3,0,2,1:T(8,128)(2,1)S(1)}, u32[]{:S(2)}, u32[]{:S(2)}) async-start(bf16[128,4,4,128]{3,0,2,1:T(8,128)(2,1)} %copy.47), calls=%async_computation | async-start | bytes 1048576 | tf_op jit(solution)/shard_map/all_to_all | solution.py:116
  55.1 12.7 %all-to-all-done = bf16[128,4,4,128]{3,0,2,1:T(8,128)(2,1)S(1)} async-done(((bf16[128,4,4,128]{3,0,2,1:T(8,128)(2,1)}), bf16[128,4,4,128]{3,0,2,1:T(8,128)(2,1)S(1)}, u32[]{:S(2)}, u32[]{:S(2)}) %all-to-all-start) | async-done | bytes 524320 | tf_op jit(solution)/shard_map/all_to_all | solution.py:116
  67.8 3.5 %all-to-all-start.4 = ((bf16[128,4,4,128]{3,0,2,1:T(8,128)(2,1)}), bf16[128,4,4,128]{3,0,2,1:T(8,128)(2,1)S(1)}, u32[]{:S(2)}, u32[]{:S(2)}) async-start(bf16[128,4,4,128]{3,0,2,1:T(8,128)(2,1)} %copy.61), calls=%async_computation.4 | async-start | bytes 1048576 | tf_op jit(solution)/shard_map/all_to_all | solution.py:125
  71.4 13.9 %all-to-all-done.4 = bf16[128,4,4,128]{3,0,2,1:T(8,128)(2,1)S(1)} async-done(((bf16[128,4,4,128]{3,0,2,1:T(8,128)(2,1)}), bf16[128,4,4,128]{3,0,2,1:T(8,128)(2,1)S(1)}, u32[]{:S(2)}, u32[]{:S(2)}) %all-to-all-start.4) | async-done | bytes 524320 | tf_op jit(solution)/shard_map/all_to_all | solution.py:125
  88.3 1.8 %select_convert_fusion = bf16[4,512,512]{2,1,0:T(8,128)(2,1)S(1)} fusion(bf16[512,4,128]{2,0,1:T(8,128)(2,1)} %copy-done, bf16[512,4,128]{2,0,1:T(8,128)(2,1)S(1)} %bitcast.115, pred[512,512]{1,0:T(8,128)(4,1)S(1)} %iota_compare_fusion), kind=kOutput, calls=%fused_computation | convolution fusion | flops 270532608 | bytes 3407872 | tf_op jit(solution)/shard_map/tnd,snd->nts/dot_general | solution.py:33
  90.2 1.7 convolution_bitcast_fusion.1
  91.9 2.0 %multiply_reduce_fusion.1 = bf16[4,128,128]{2,1,0:T(8,128)(2,1)S(1)} fusion(f32[8,4,128,128]{3,2,1,0:T(8,128)} %bitcast.123, f32[8]{0:T(128)S(1)} %compare_convert_fusion.1), kind=kLoop, calls=%fused_computation.3 | loop fusion | flops 983040 | bytes 2228256 | tf_op jit(solution)/shard_map/reduce_sum | solution.py:96
  94.3 1.2 copy.64
  95.5 4.1 %all-to-all-start.5 = ((bf16[512,1,4,128]{3,2,1,0:T(4,128)(2,1)}), bf16[512,1,4,128]{3,2,1,0:T(4,128)(2,1)}, u32[]{:S(2)}, u32[]{:S(2)}) async-start(bf16[512,1,4,128]{3,2,1,0:T(4,128)(2,1)} %copy.64), calls=%async_computation.5 | async-start | bytes 1048576 | tf_op jit(solution)/shard_map/all_to_all | solution.py:132
  99.7 2.9 %convolution_bitcast_fusion = f32[512,4,128]{2,0,1:T(8,128)} fusion(bf16[4,512,512]{2,1,0:T(8,128)(2,1)S(1)} %select_convert_fusion, bf16[512,4,128]{2,0,1:T(8,128)(2,1)} %bitcast.119), kind=kOutput, calls=%fused_computation.4 | convolution fusion | flops 268435456 | bytes 3670016 | tf_op jit(solution)/shard_map/nts,tnd->snd/dot_general | solution.py:55
  102.6 12.0 %all-gather.7.cloned.1.call-done = f32[32,128,128]{2,1,0:T(8,128)} async-done(((f32[4,128,128]{2,1,0:T(8,128)}), f32[32,128,128]{2,1,0:T(8,128)}) %all-gather.7.cloned.1.call-update) | async-done | bytes 2097168 | tf_op jit(solution)/shard_map/all_gather | solution.py:91
  114.6 1.8 %multiply_reduce_fusion = bf16[4,128,128]{2,1,0:T(8,128)(2,1)S(1)} fusion(f32[8,4,128,128]{3,2,1,0:T(8,128)} %bitcast.124, f32[8]{0:T(128)S(1)} %compare_convert_fusion), kind=kLoop, calls=%fused_computation.2 | loop fusion | flops 983040 | bytes 2228256 | tf_op jit(solution)/shard_map/reduce_sum | solution.py:97
  116.7 1.2 copy.70
  117.9 4.6 %all-to-all-start.6 = ((bf16[512,1,4,128]{3,2,1,0:T(4,128)(2,1)}), bf16[512,1,4,128]{3,2,1,0:T(4,128)(2,1)}, u32[]{:S(2)}, u32[]{:S(2)}) async-start(bf16[512,1,4,128]{3,2,1,0:T(4,128)(2,1)} %copy.70), calls=%async_computation.6 | async-start | bytes 1048576 | tf_op jit(solution)/shard_map/all_to_all | solution.py:133
  122.5 1.9 %select_convert_fusion.1 = bf16[4,512,512]{2,1,0:T(8,128)(2,1)S(1)} fusion(bf16[512,4,128]{2,0,1:T(8,128)(2,1)} %bitcast.120, bf16[512,4,128]{2,0,1:T(8,128)(2,1)S(1)} %bitcast.112, pred[512,512]{1,0:T(8,128)(4,1)} %copy-done.10), kind=kOutput, calls=%fused_computation.1 | convolution fusion | flops 270532608 | bytes 3407872 | tf_op jit(solution)/shard_map/tnd,snd->nts/dot_general | solution.py:29
  125.7 1.2 copy.58
  126.9 10.6 %all-to-all-done.6 = bf16[512,1,4,128]{3,2,1,0:T(4,128)(2,1)} async-done(((bf16[512,1,4,128]{3,2,1,0:T(4,128)(2,1)}), bf16[512,1,4,128]{3,2,1,0:T(4,128)(2,1)}, u32[]{:S(2)}, u32[]{:S(2)}) %all-to-all-start.6) | async-done | bytes 524320 | tf_op jit(solution)/shard_map/all_to_all | solution.py:133
  137.5 4.1 %all-to-all-start.3 = ((bf16[512,1,4,128]{3,2,1,0:T(4,128)(2,1)}), bf16[512,1,4,128]{3,2,1,0:T(4,128)(2,1)}, u32[]{:S(2)}, u32[]{:S(2)}) async-start(bf16[512,1,4,128]{3,2,1,0:T(4,128)(2,1)} %copy.58), calls=%async_computation.3 | async-start | bytes 1048576 | tf_op jit(solution)/shard_map/all_to_all | solution.py:131
  143.5 12.2 %all-to-all-done.3 = bf16[512,1,4,128]{3,2,1,0:T(4,128)(2,1)} async-done(((bf16[512,1,4,128]{3,2,1,0:T(4,128)(2,1)}), bf16[512,1,4,128]{3,2,1,0:T(4,128)(2,1)}, u32[]{:S(2)}, u32[]{:S(2)}) %all-to-all-start.3) | async-done | bytes 524320 | tf_op jit(solution)/shard_map/all_to_all | solution.py:131
  155.8 3.6 %all-to-all-start.7 = ((bf16[512,1,4,128]{3,2,1,0:T(4,128)(2,1)}), bf16[512,1,4,128]{3,2,1,0:T(4,128)(2,1)S(1)}, u32[]{:S(2)}, u32[]{:S(2)}) async-start(bf16[512,1,4,128]{3,2,1,0:T(4,128)(2,1)} %copy.73), calls=%async_computation.7 | async-start | bytes 1048576 | tf_op jit(solution)/shard_map/all_to_all | solution.py:134
  159.4 1.2 copy.65
  160.7 1.2 reshape.143
  161.8 1.2 copy.71
  163.1 1.2 reshape.144
  164.2 1.2 copy.59
  165.5 1.2 reshape.141
  166.6 6.6 %all-to-all-done.7 = bf16[512,1,4,128]{3,2,1,0:T(4,128)(2,1)S(1)} async-done(((bf16[512,1,4,128]{3,2,1,0:T(4,128)(2,1)}), bf16[512,1,4,128]{3,2,1,0:T(4,128)(2,1)S(1)}, u32[]{:S(2)}, u32[]{:S(2)}) %all-to-all-start.7) | async-done | bytes 524320 | tf_op jit(solution)/shard_map/all_to_all | solution.py:134
  (56 shorter events, 14.4 us)
Async XLA Ops:
  7.2 8.7 %copy-start.7 = (bf16[128,2048]{1,0:T(8,128)(2,1)S(1)}, bf16[128,2048]{1,0:T(8,128)(2,1)}, u32[]{:S(2)}) copy-start(bf16[128,2048]{1,0:T(8,128)(2,1)} %param.14) | copy-start | bytes 1572868
  9.6 20.8 %all-to-all-start.1 = ((bf16[128,4,4,128]{3,0,2,1:T(8,128)(2,1)}), bf16[128,4,4,128]{3,0,2,1:T(8,128)(2,1)S(1)}, u32[]{:S(2)}, u32[]{:S(2)}) async-start(bf16[128,4,4,128]{3,0,2,1:T(8,128)(2,1)} %copy.50), calls=%async_computation.1 | async-start | bytes 1048576 | tf_op jit(solution)/shard_map/all_to_all | solution.py:119
  30.4 17.5 %all-to-all-start.2 = ((bf16[128,4,4,128]{3,0,2,1:T(8,128)(2,1)}), bf16[128,4,4,128]{3,0,2,1:T(8,128)(2,1)S(1)}, u32[]{:S(2)}, u32[]{:S(2)}) async-start(bf16[128,4,4,128]{3,0,2,1:T(8,128)(2,1)} %copy.53), calls=%async_computation.2 | async-start | bytes 1048576 | tf_op jit(solution)/shard_map/all_to_all | solution.py:122
  33.9 15.2 %copy-start.8 = (bf16[128,2048]{1,0:T(8,128)(2,1)S(1)}, bf16[128,2048]{1,0:T(8,128)(2,1)}, u32[]{:S(2)}) copy-start(bf16[128,2048]{1,0:T(8,128)(2,1)} %param.12) | copy-start | bytes 1572868
  33.9 58.0 %all-gather.5.cloned.1.call-start = ((), (), s32[]{:S(2)}) async-start(), calls=%async_computation.8 | async-start | bytes 2359296 | tf_op jit(solution)/shard_map/all_gather | solution.py:90
  47.9 5.9 %copy-start.9 = (bf16[128,2048]{1,0:T(8,128)(2,1)S(1)}, bf16[128,2048]{1,0:T(8,128)(2,1)}, u32[]{:S(2)}) copy-start(bf16[128,2048]{1,0:T(8,128)(2,1)} %param.15) | copy-start | bytes 1572868
  50.3 17.5 %all-to-all-start = ((bf16[128,4,4,128]{3,0,2,1:T(8,128)(2,1)}), bf16[128,4,4,128]{3,0,2,1:T(8,128)(2,1)S(1)}, u32[]{:S(2)}, u32[]{:S(2)}) async-start(bf16[128,4,4,128]{3,0,2,1:T(8,128)(2,1)} %copy.47), calls=%async_computation | async-start | bytes 1048576 | tf_op jit(solution)/shard_map/all_to_all | solution.py:116
  67.8 17.5 %all-to-all-start.4 = ((bf16[128,4,4,128]{3,0,2,1:T(8,128)(2,1)}), bf16[128,4,4,128]{3,0,2,1:T(8,128)(2,1)S(1)}, u32[]{:S(2)}, u32[]{:S(2)}) async-start(bf16[128,4,4,128]{3,0,2,1:T(8,128)(2,1)} %copy.61), calls=%async_computation.4 | async-start | bytes 1048576 | tf_op jit(solution)/shard_map/all_to_all | solution.py:125
  71.3 43.3 %all-gather.7.cloned.1.call-start = ((), (), s32[]{:S(2)}) async-start(), calls=%async_computation.9 | async-start | bytes 2359296 | tf_op jit(solution)/shard_map/all_gather | solution.py:91
  71.4 14.3 %copy-start.3 = (bf16[4,128,1,4,128]{4,1,0,3,2:T(8,128)(2,1)}, bf16[4,128,1,4,128]{4,1,0,3,2:T(8,128)(2,1)S(1)}, u32[]{:S(2)}) copy-start(bf16[4,128,1,4,128]{4,1,0,3,2:T(8,128)(2,1)S(1)} %copy.48) | copy-start | bytes 1572868
  85.7 0.8 copy-start
  87.6 0.7 copy-start.10
  91.9 2.0 %copy-start.1 = (bf16[512,4,128]{2,0,1:T(8,128)(2,1)S(1)}, bf16[512,4,128]{2,0,1:T(8,128)(2,1)}, u32[]{:S(2)}) copy-start(bf16[512,4,128]{2,0,1:T(8,128)(2,1)} %copy-done) | copy-start | bytes 1572868
  91.9 2.1 %copy-start.6 = (f32[512,4,128]{2,0,1:T(8,128)S(1)}, f32[512,4,128]{2,0,1:T(8,128)}, u32[]{:S(2)}) copy-start(f32[512,4,128]{2,0,1:T(8,128)} %convolution_bitcast_fusion.1) | copy-start | bytes 3145732
  95.5 22.4 %all-to-all-start.5 = ((bf16[512,1,4,128]{3,2,1,0:T(4,128)(2,1)}), bf16[512,1,4,128]{3,2,1,0:T(4,128)(2,1)}, u32[]{:S(2)}, u32[]{:S(2)}) async-start(bf16[512,1,4,128]{3,2,1,0:T(4,128)(2,1)} %copy.64), calls=%async_computation.5 | async-start | bytes 1048576 | tf_op jit(solution)/shard_map/all_to_all | solution.py:132
  102.6 13.8 %copy-start.5 = (f32[512,4,128]{2,0,1:T(8,128)S(1)}, f32[512,4,128]{2,0,1:T(8,128)}, u32[]{:S(2)}) copy-start(f32[512,4,128]{2,0,1:T(8,128)} %convolution_bitcast_fusion) | copy-start | bytes 3145732
  117.9 19.6 %all-to-all-start.6 = ((bf16[512,1,4,128]{3,2,1,0:T(4,128)(2,1)}), bf16[512,1,4,128]{3,2,1,0:T(4,128)(2,1)}, u32[]{:S(2)}, u32[]{:S(2)}) async-start(bf16[512,1,4,128]{3,2,1,0:T(4,128)(2,1)} %copy.70), calls=%async_computation.6 | async-start | bytes 1048576 | tf_op jit(solution)/shard_map/all_to_all | solution.py:133
  124.4 1.0 copy-start.4
  125.4 16.2 %copy-start.2 = (bf16[512,4,128]{2,0,1:T(8,128)(2,1)S(1)}, bf16[512,4,128]{2,0,1:T(8,128)(2,1)}, u32[]{:S(2)}) copy-start(bf16[512,4,128]{2,0,1:T(8,128)(2,1)} %copy-done) | copy-start | bytes 1572868
  137.5 18.3 %all-to-all-start.3 = ((bf16[512,1,4,128]{3,2,1,0:T(4,128)(2,1)}), bf16[512,1,4,128]{3,2,1,0:T(4,128)(2,1)}, u32[]{:S(2)}, u32[]{:S(2)}) async-start(bf16[512,1,4,128]{3,2,1,0:T(4,128)(2,1)} %copy.58), calls=%async_computation.3 | async-start | bytes 1048576 | tf_op jit(solution)/shard_map/all_to_all | solution.py:131
  155.8 17.5 %all-to-all-start.7 = ((bf16[512,1,4,128]{3,2,1,0:T(4,128)(2,1)}), bf16[512,1,4,128]{3,2,1,0:T(4,128)(2,1)S(1)}, u32[]{:S(2)}, u32[]{:S(2)}) async-start(bf16[512,1,4,128]{3,2,1,0:T(4,128)(2,1)} %copy.73), calls=%async_computation.7 | async-start | bytes 1048576 | tf_op jit(solution)/shard_map/all_to_all | solution.py:134
Sparse Core Ops, SparseCore 0:
  49.2 26.8 all-gather.4
  87.7 26.8 all-gather.6
where the time goes:
time: 182 us; the launch traced here: 181 us
  waiting for transfers between devices  95.1 us (52%)
  starting transfers between devices  33.4 us (18%)
  local copies, waits for them, and re-layouts  21.6 us (12%)
  between operations  14.4 us (8%)
  matrix products  12.8 us (7%)
  other arithmetic  4.16 us (2%)
    all_to_all x1, waiting for transfers between devices, shards(): lax.all_to_all(split_heads(values, group_count), 'head', split_axis=1, co...  13.9 us
    all_to_all x1, waiting for transfers between devices, shards(): lax.all_to_all(split_heads(out_grad, group_count), 'head', split_axis=1,...  13.9 us
    all_to_all x1, waiting for transfers between devices, shards(): lax.all_to_all(split_heads(keys, group_count), 'head', split_axis=1, conc...  13.2 us
    all_to_all x1, waiting for transfers between devices, shards(): lax.all_to_all(split_heads(queries, group_count), 'head', split_axis=1, c...  12.7 us
    all_to_all x1, waiting for transfers between devices, shards(): lax.all_to_all(results[0], 'head', split_axis=0, concat_axis=1, tiled=True)  12.2 us
    all_gather x1, waiting for transfers between devices, attend(): lax.all_gather(back_local[None], 'span', axis=0, tiled=True)  12 us
    all_to_all x1, waiting for transfers between devices, shards(): lax.all_to_all(results[2], 'head', split_axis=0, concat_axis=1, tiled=True)  10.6 us
    all_to_all x1, waiting for transfers between devices, shards(): lax.all_to_all(results[3], 'head', split_axis=0, concat_axis=1, tiled=True)  6.61 us
  transfers between devices with their start and end apart: 10, of which 8 were waited for; matrix products, arithmetic and copies ran while one was open for 18% of the time, Pallas kernels for 0%

commit v1 on v0

--- a/solution.py
+++ b/solution.py
@@ -111,6 +111,15 @@
 
 def shards(queries, keys, values, out_grad):
     group_count = lax.axis_size("head")
+    derive_case = lambda a0, chip_axis: jnp.concatenate(
+        lax.all_to_all(
+            jnp.stack(jnp.split(a0, lax.axis_size(chip_axis), axis=1)),
+            chip_axis,
+            split_axis=0,
+            concat_axis=0,
+        ),
+        axis=0,
+    )
     results = attend(
         (
             lax.all_to_all(
@@ -122,9 +131,7 @@
             lax.all_to_all(
                 split_heads(values, group_count), "head", split_axis=1, concat_axis=0, tiled=True
             ),
-            lax.all_to_all(
-                split_heads(out_grad, group_count), "head", split_axis=1, concat_axis=0, tiled=True
-            ),
+            derive_case(split_heads(out_grad, group_count), "head"),
         )
     )
     returned = (

time: 182 us -> 182 us (level)
    reshape x4 -> x3, local copies, waits for them, and re-layouts: 4.05 us -> 3.04 us  [split_heads(): matrix.reshape(matrix.shape[0], group_count, HEADS // group_count, DH)]
where the time goes in v1:
time: 182 us; the launch traced here: 181 us
  waiting for transfers between devices  95 us (52%)
  starting transfers between devices  33.4 us (18%)
  local copies, waits for them, and re-layouts  21.7 us (12%)
  between operations  14.4 us (8%)
  matrix products  12.8 us (7%)
  other arithmetic  4.14 us (2%)
    all_to_all x1, waiting for transfers between devices, shards(): lax.all_to_all(split_heads(values, group_count), 'head', split_axis=1, co...  13.9 us
    all_to_all x1, waiting for transfers between devices, shards(): lax.all_to_all(jnp.stack(jnp.split(a0, lax.axis_size(chip_axis), axis=1))...  13.9 us
    all_to_all x1, waiting for transfers between devices, shards(): lax.all_to_all(split_heads(keys, group_count), 'head', split_axis=1, conc...  13.2 us
    all_to_all x1, waiting for transfers between devices, shards(): lax.all_to_all(split_heads(queries, group_count), 'head', split_axis=1, c...  12.6 us
    all_to_all x1, waiting for transfers between devices, shards(): lax.all_to_all(results[0], 'head', split_axis=0, concat_axis=1, tiled=True)  12.2 us
    all_gather x1, waiting for transfers between devices, attend(): lax.all_gather(back_local[None], 'span', axis=0, tiled=True)  12 us
    all_to_all x1, waiting for transfers between devices, shards(): lax.all_to_all(results[2], 'head', split_axis=0, concat_axis=1, tiled=True)  10.6 us
    all_to_all x1, waiting for transfers between devices, shards(): lax.all_to_all(results[3], 'head', split_axis=0, concat_axis=1, tiled=True)  6.61 us
  transfers between devices with their start and end apart: 10, of which 8 were waited for; matrix products, arithmetic and copies ran while one was open for 18% of the time, Pallas kernels for 0%

profile of v1, /device:TPU:0, one launch (start us, length us, event | category | flops | bytes accessed | tf_op | source)
XLA Modules:
  0.0 181.4 jit_solution(4253772384939842019)
XLA Ops:
  7.2 1.4 copy.52
  9.6 6.3 %all-to-all-start.1 = ((bf16[128,4,4,128]{3,0,2,1:T(8,128)(2,1)}), bf16[128,4,4,128]{3,0,2,1:T(8,128)(2,1)S(1)}, u32[]{:S(2)}, u32[]{:S(2)}) async-start(bf16[128,4,4,128]{3,0,2,1:T(8,128)(2,1)} %copy.53), calls=%async_computation.1 | async-start | bytes 1048576 | tf_op jit(solution)/shard_map/all_to_all | solution.py:128
  17.2 13.2 %all-to-all-done.1 = bf16[128,4,4,128]{3,0,2,1:T(8,128)(2,1)S(1)} async-done(((bf16[128,4,4,128]{3,0,2,1:T(8,128)(2,1)}), bf16[128,4,4,128]{3,0,2,1:T(8,128)(2,1)S(1)}, u32[]{:S(2)}, u32[]{:S(2)}) %all-to-all-start.1) | async-done | bytes 524320 | tf_op jit(solution)/shard_map/all_to_all | solution.py:128
  30.4 3.5 %all-to-all-start.2 = ((bf16[128,4,4,128]{3,0,2,1:T(8,128)(2,1)}), bf16[128,4,4,128]{3,0,2,1:T(8,128)(2,1)S(1)}, u32[]{:S(2)}, u32[]{:S(2)}) async-start(bf16[128,4,4,128]{3,0,2,1:T(8,128)(2,1)} %copy.56), calls=%async_computation.2 | async-start | bytes 1048576 | tf_op jit(solution)/shard_map/all_to_all | solution.py:131
  34.0 13.9 %all-to-all-done.2 = bf16[128,4,4,128]{3,0,2,1:T(8,128)(2,1)S(1)} async-done(((bf16[128,4,4,128]{3,0,2,1:T(8,128)(2,1)}), bf16[128,4,4,128]{3,0,2,1:T(8,128)(2,1)S(1)}, u32[]{:S(2)}, u32[]{:S(2)}) %all-to-all-start.2) | async-done | bytes 524320 | tf_op jit(solution)/shard_map/all_to_all | solution.py:131
  50.3 3.5 %all-to-all-start = ((bf16[128,4,4,128]{3,0,2,1:T(8,128)(2,1)}), bf16[128,4,4,128]{3,0,2,1:T(8,128)(2,1)S(1)}, u32[]{:S(2)}, u32[]{:S(2)}) async-start(bf16[128,4,4,128]{3,0,2,1:T(8,128)(2,1)} %copy.50), calls=%async_computation | async-start | bytes 1048576 | tf_op jit(solution)/shard_map/all_to_all | solution.py:125
  55.2 12.6 %all-to-all-done = bf16[128,4,4,128]{3,0,2,1:T(8,128)(2,1)S(1)} async-done(((bf16[128,4,4,128]{3,0,2,1:T(8,128)(2,1)}), bf16[128,4,4,128]{3,0,2,1:T(8,128)(2,1)S(1)}, u32[]{:S(2)}, u32[]{:S(2)}) %all-to-all-start) | async-done | bytes 524320 | tf_op jit(solution)/shard_map/all_to_all | solution.py:125
  67.8 3.5 %all-to-all-start.4 = ((bf16[4,128,1,4,128]{4,1,3,2,0:T(8,128)(2,1)}), bf16[4,128,1,4,128]{4,1,3,2,0:T(8,128)(2,1)S(1)}, u32[]{:S(2)}, u32[]{:S(2)}) async-start(bf16[4,128,1,4,128]{4,1,3,2,0:T(8,128)(2,1)} %copy.64), calls=%async_computation.4 | async-start | bytes 1048576 | tf_op jit(solution)/shard_map/all_to_all | solution.py:115
  71.4 13.9 %all-to-all-done.4 = bf16[4,128,1,4,128]{4,1,3,2,0:T(8,128)(2,1)S(1)} async-done(((bf16[4,128,1,4,128]{4,1,3,2,0:T(8,128)(2,1)}), bf16[4,128,1,4,128]{4,1,3,2,0:T(8,128)(2,1)S(1)}, u32[]{:S(2)}, u32[]{:S(2)}) %all-to-all-start.4) | async-done | bytes 524320 | tf_op jit(solution)/shard_map/all_to_all | solution.py:115
  88.3 1.8 select_convert_fusion
  90.1 1.7 convolution_bitcast_fusion.1
  91.8 2.0 %multiply_reduce_fusion.1 = bf16[4,128,128]{2,1,0:T(8,128)(2,1)S(1)} fusion(f32[8,4,128,128]{3,2,1,0:T(8,128)} %bitcast.126, f32[8]{0:T(128)S(1)} %compare_convert_fusion.1), kind=kLoop, calls=%fused_computation.3 | loop fusion | flops 983040 | bytes 2228256 | tf_op jit(solution)/shard_map/reduce_sum | solution.py:96
  94.2 1.2 copy.67
  95.4 4.1 %all-to-all-start.5 = ((bf16[512,1,4,128]{3,2,1,0:T(4,128)(2,1)}), bf16[512,1,4,128]{3,2,1,0:T(4,128)(2,1)}, u32[]{:S(2)}, u32[]{:S(2)}) async-start(bf16[512,1,4,128]{3,2,1,0:T(4,128)(2,1)} %copy.67), calls=%async_computation.5 | async-start | bytes 1048576 | tf_op jit(solution)/shard_map/all_to_all | solution.py:139
  99.6 2.9 %convolution_bitcast_fusion = f32[512,4,128]{2,0,1:T(8,128)} fusion(bf16[4,512,512]{2,1,0:T(8,128)(2,1)S(1)} %select_convert_fusion, bf16[512,4,128]{2,0,1:T(8,128)(2,1)} %bitcast.122), kind=kOutput, calls=%fused_computation.4 | convolution fusion | flops 268435456 | bytes 3670016 | tf_op jit(solution)/shard_map/nts,tnd->snd/dot_general | solution.py:55
  102.5 12.0 %all-gather.7.cloned.1.call-done = f32[32,128,128]{2,1,0:T(8,128)} async-done(((f32[4,128,128]{2,1,0:T(8,128)}), f32[32,128,128]{2,1,0:T(8,128)}) %all-gather.7.cloned.1.call-update) | async-done | bytes 2097168 | tf_op jit(solution)/shard_map/all_gather | solution.py:91
  114.5 1.8 %multiply_reduce_fusion = bf16[4,128,128]{2,1,0:T(8,128)(2,1)S(1)} fusion(f32[8,4,128,128]{3,2,1,0:T(8,128)} %bitcast.127, f32[8]{0:T(128)S(1)} %compare_convert_fusion), kind=kLoop, calls=%fused_computation.2 | loop fusion | flops 983040 | bytes 2228256 | tf_op jit(solution)/shard_map/reduce_sum | solution.py:97
  116.6 1.2 copy.73
  117.8 4.6 %all-to-all-start.6 = ((bf16[512,1,4,128]{3,2,1,0:T(4,128)(2,1)}), bf16[512,1,4,128]{3,2,1,0:T(4,128)(2,1)}, u32[]{:S(2)}, u32[]{:S(2)}) async-start(bf16[512,1,4,128]{3,2,1,0:T(4,128)(2,1)} %copy.73), calls=%async_computation.6 | async-start | bytes 1048576 | tf_op jit(solution)/shard_map/all_to_all | solution.py:140
  122.4 1.9 %select_convert_fusion.1 = bf16[4,512,512]{2,1,0:T(8,128)(2,1)S(1)} fusion(bf16[512,4,128]{2,0,1:T(8,128)(2,1)} %bitcast.123, bf16[512,4,128]{2,0,1:T(8,128)(2,1)S(1)} %bitcast.115, pred[512,512]{1,0:T(8,128)(4,1)} %copy-done.10), kind=kOutput, calls=%fused_computation.1 | convolution fusion | flops 270532608 | bytes 3407872 | tf_op jit(solution)/shard_map/tnd,snd->nts/dot_general | solution.py:29
  125.6 1.2 copy.61
  126.8 10.6 %all-to-all-done.6 = bf16[512,1,4,128]{3,2,1,0:T(4,128)(2,1)} async-done(((bf16[512,1,4,128]{3,2,1,0:T(4,128)(2,1)}), bf16[512,1,4,128]{3,2,1,0:T(4,128)(2,1)}, u32[]{:S(2)}, u32[]{:S(2)}) %all-to-all-start.6) | async-done | bytes 524320 | tf_op jit(solution)/shard_map/all_to_all | solution.py:140
  137.4 4.2 %all-to-all-start.3 = ((bf16[512,1,4,128]{3,2,1,0:T(4,128)(2,1)}), bf16[512,1,4,128]{3,2,1,0:T(4,128)(2,1)}, u32[]{:S(2)}, u32[]{:S(2)}) async-start(bf16[512,1,4,128]{3,2,1,0:T(4,128)(2,1)} %copy.61), calls=%async_computation.3 | async-start | bytes 1048576 | tf_op jit(solution)/shard_map/all_to_all | solution.py:138
  143.4 12.2 %all-to-all-done.3 = bf16[512,1,4,128]{3,2,1,0:T(4,128)(2,1)} async-done(((bf16[512,1,4,128]{3,2,1,0:T(4,128)(2,1)}), bf16[512,1,4,128]{3,2,1,0:T(4,128)(2,1)}, u32[]{:S(2)}, u32[]{:S(2)}) %all-to-all-start.3) | async-done | bytes 524320 | tf_op jit(solution)/shard_map/all_to_all | solution.py:138
  155.7 3.6 %all-to-all-start.7 = ((bf16[512,1,4,128]{3,2,1,0:T(4,128)(2,1)}), bf16[512,1,4,128]{3,2,1,0:T(4,128)(2,1)S(1)}, u32[]{:S(2)}, u32[]{:S(2)}) async-start(bf16[512,1,4,128]{3,2,1,0:T(4,128)(2,1)} %copy.76), calls=%async_computation.7 | async-start | bytes 1048576 | tf_op jit(solution)/shard_map/all_to_all | solution.py:141
  159.3 1.2 copy.68
  160.6 1.2 reshape.140
  161.7 1.2 copy.74
  163.0 1.2 reshape.141
  164.1 1.2 copy.62
  165.4 1.2 reshape.138
  166.5 6.6 %all-to-all-done.7 = bf16[512,1,4,128]{3,2,1,0:T(4,128)(2,1)S(1)} async-done(((bf16[512,1,4,128]{3,2,1,0:T(4,128)(2,1)}), bf16[512,1,4,128]{3,2,1,0:T(4,128)(2,1)S(1)}, u32[]{:S(2)}, u32[]{:S(2)}) %all-to-all-start.7) | async-done | bytes 524320 | tf_op jit(solution)/shard_map/all_to_all | solution.py:141
  (57 shorter events, 14.4 us)
Async XLA Ops:
  7.2 8.7 %copy-start.7 = (bf16[128,2048]{1,0:T(8,128)(2,1)S(1)}, bf16[128,2048]{1,0:T(8,128)(2,1)}, u32[]{:S(2)}) copy-start(bf16[128,2048]{1,0:T(8,128)(2,1)} %param.14) | copy-start | bytes 1572868
  9.6 20.8 %all-to-all-start.1 = ((bf16[128,4,4,128]{3,0,2,1:T(8,128)(2,1)}), bf16[128,4,4,128]{3,0,2,1:T(8,128)(2,1)S(1)}, u32[]{:S(2)}, u32[]{:S(2)}) async-start(bf16[128,4,4,128]{3,0,2,1:T(8,128)(2,1)} %copy.53), calls=%async_computation.1 | async-start | bytes 1048576 | tf_op jit(solution)/shard_map/all_to_all | solution.py:128
  30.4 17.5 %all-to-all-start.2 = ((bf16[128,4,4,128]{3,0,2,1:T(8,128)(2,1)}), bf16[128,4,4,128]{3,0,2,1:T(8,128)(2,1)S(1)}, u32[]{:S(2)}, u32[]{:S(2)}) async-start(bf16[128,4,4,128]{3,0,2,1:T(8,128)(2,1)} %copy.56), calls=%async_computation.2 | async-start | bytes 1048576 | tf_op jit(solution)/shard_map/all_to_all | solution.py:131
  33.9 15.1 %copy-start.8 = (bf16[128,2048]{1,0:T(8,128)(2,1)S(1)}, bf16[128,2048]{1,0:T(8,128)(2,1)}, u32[]{:S(2)}) copy-start(bf16[128,2048]{1,0:T(8,128)(2,1)} %param.12) | copy-start | bytes 1572868
  33.9 57.9 %all-gather.5.cloned.1.call-start = ((), (), s32[]{:S(2)}) async-start(), calls=%async_computation.8 | async-start | bytes 2359296 | tf_op jit(solution)/shard_map/all_gather | solution.py:90
  47.9 5.9 %copy-start.9 = (bf16[128,2048]{1,0:T(8,128)(2,1)S(1)}, bf16[128,2048]{1,0:T(8,128)(2,1)}, u32[]{:S(2)}) copy-start(bf16[128,2048]{1,0:T(8,128)(2,1)} %param.15) | copy-start | bytes 1572868
  50.3 17.5 %all-to-all-start = ((bf16[128,4,4,128]{3,0,2,1:T(8,128)(2,1)}), bf16[128,4,4,128]{3,0,2,1:T(8,128)(2,1)S(1)}, u32[]{:S(2)}, u32[]{:S(2)}) async-start(bf16[128,4,4,128]{3,0,2,1:T(8,128)(2,1)} %copy.50), calls=%async_computation | async-start | bytes 1048576 | tf_op jit(solution)/shard_map/all_to_all | solution.py:125
  67.8 17.5 %all-to-all-start.4 = ((bf16[4,128,1,4,128]{4,1,3,2,0:T(8,128)(2,1)}), bf16[4,128,1,4,128]{4,1,3,2,0:T(8,128)(2,1)S(1)}, u32[]{:S(2)}, u32[]{:S(2)}) async-start(bf16[4,128,1,4,128]{4,1,3,2,0:T(8,128)(2,1)} %copy.64), calls=%async_computation.4 | async-start | bytes 1048576 | tf_op jit(solution)/shard_map/all_to_all | solution.py:115
  71.3 43.2 %all-gather.7.cloned.1.call-start = ((), (), s32[]{:S(2)}) async-start(), calls=%async_computation.9 | async-start | bytes 2359296 | tf_op jit(solution)/shard_map/all_gather | solution.py:91
  71.4 16.0 %copy-start.3 = (bf16[4,128,1,4,128]{4,1,0,3,2:T(8,128)(2,1)}, bf16[4,128,1,4,128]{4,1,0,3,2:T(8,128)(2,1)S(1)}, u32[]{:S(2)}) copy-start(bf16[4,128,1,4,128]{4,1,0,3,2:T(8,128)(2,1)S(1)} %copy.51) | copy-start | bytes 1572868
  85.6 0.8 copy-start
  87.5 0.7 copy-start.10
  91.8 2.0 %copy-start.1 = (bf16[512,4,128]{2,0,1:T(8,128)(2,1)S(1)}, bf16[512,4,128]{2,0,1:T(8,128)(2,1)}, u32[]{:S(2)}) copy-start(bf16[512,4,128]{2,0,1:T(8,128)(2,1)} %copy-done) | copy-start | bytes 1572868
  91.8 2.1 %copy-start.6 = (f32[512,4,128]{2,0,1:T(8,128)S(1)}, f32[512,4,128]{2,0,1:T(8,128)}, u32[]{:S(2)}) copy-start(f32[512,4,128]{2,0,1:T(8,128)} %convolution_bitcast_fusion.1) | copy-start | bytes 3145732
  95.4 22.4 %all-to-all-start.5 = ((bf16[512,1,4,128]{3,2,1,0:T(4,128)(2,1)}), bf16[512,1,4,128]{3,2,1,0:T(4,128)(2,1)}, u32[]{:S(2)}, u32[]{:S(2)}) async-start(bf16[512,1,4,128]{3,2,1,0:T(4,128)(2,1)} %copy.67), calls=%async_computation.5 | async-start | bytes 1048576 | tf_op jit(solution)/shard_map/all_to_all | solution.py:139
  102.5 13.8 %copy-start.5 = (f32[512,4,128]{2,0,1:T(8,128)S(1)}, f32[512,4,128]{2,0,1:T(8,128)}, u32[]{:S(2)}) copy-start(f32[512,4,128]{2,0,1:T(8,128)} %convolution_bitcast_fusion) | copy-start | bytes 3145732
  117.8 19.6 %all-to-all-start.6 = ((bf16[512,1,4,128]{3,2,1,0:T(4,128)(2,1)}), bf16[512,1,4,128]{3,2,1,0:T(4,128)(2,1)}, u32[]{:S(2)}, u32[]{:S(2)}) async-start(bf16[512,1,4,128]{3,2,1,0:T(4,128)(2,1)} %copy.73), calls=%async_computation.6 | async-start | bytes 1048576 | tf_op jit(solution)/shard_map/all_to_all | solution.py:140
  124.3 1.0 copy-start.4
  125.3 16.2 %copy-start.2 = (bf16[512,4,128]{2,0,1:T(8,128)(2,1)S(1)}, bf16[512,4,128]{2,0,1:T(8,128)(2,1)}, u32[]{:S(2)}) copy-start(bf16[512,4,128]{2,0,1:T(8,128)(2,1)} %copy-done) | copy-start | bytes 1572868
  137.4 18.3 %all-to-all-start.3 = ((bf16[512,1,4,128]{3,2,1,0:T(4,128)(2,1)}), bf16[512,1,4,128]{3,2,1,0:T(4,128)(2,1)}, u32[]{:S(2)}, u32[]{:S(2)}) async-start(bf16[512,1,4,128]{3,2,1,0:T(4,128)(2,1)} %copy.61), calls=%async_computation.3 | async-start | bytes 1048576 | tf_op jit(solution)/shard_map/all_to_all | solution.py:138
  155.7 17.5 %all-to-all-start.7 = ((bf16[512,1,4,128]{3,2,1,0:T(4,128)(2,1)}), bf16[512,1,4,128]{3,2,1,0:T(4,128)(2,1)S(1)}, u32[]{:S(2)}, u32[]{:S(2)}) async-start(bf16[512,1,4,128]{3,2,1,0:T(4,128)(2,1)} %copy.76), calls=%async_computation.7 | async-start | bytes 1048576 | tf_op jit(solution)/shard_map/all_to_all | solution.py:141
Sparse Core Ops, SparseCore 0:
  49.1 26.8 all-gather.4
  87.5 26.8 all-gather.6
